TPU v7x, 32 devices: a whole 2x2x4 slice. The times are simulated.
32 devices in a mesh: rows: 4 (over x, core), cols: 8 (over z, y).
Axes of the slice: x: 2, y: 2, z: 4, core: 2. Of those that a mesh axis runs over, the one named last changes fastest.
Arguments:
- pair_integrals: float32 [4096, 4096], P('rows', 'cols'), may hold values from -6 to 6
- left_factor: float32 [4096, 1024], P('rows', 'cols'), may hold values from -0.9375 to 0.9375
- core: float32 [1024, 1024], replicated, may hold values from -6 to 6
- right_factor: float32 [4096, 1024], P('cols', 'rows'), may hold values from -0.9375 to 0.9375
Outputs:
- core_next: float32 [1024, 1024], replicated
All inputs are finite; a program needn't handle non-finite values.
Results may differ from a plain program's by a relative error of at most 0.000062.
Values sent between devices are 32-bit elements; how exact they have to be, the bound alone decides.
No kernel may reach another device: no remote copies, remote signals or barrier semaphores. Data moves between devices by JAX's collectives and lax.ppermute only.
A program may use at most 128 MiB of HBM per device.

v0:
```python
import jax
import jax.numpy as jnp
from jax import lax
from jax.sharding import PartitionSpec as P


def product(left, right):
    return jnp.dot(left, right, precision=lax.Precision.HIGHEST, preferred_element_type=jnp.float32)


def shards(pair_integrals, left_factor, core, right_factor):
    left_rows = lax.all_gather(left_factor, "cols", axis=1, tiled=True)
    right_rows = lax.all_gather(right_factor, "rows", axis=1, tiled=True)
    mixed = product(core, right_rows.T)
    residual = pair_integrals - product(left_rows, mixed)
    along = product(residual, right_rows)
    local_term = product(left_rows.T, along)
    gradient = lax.psum(local_term, ("rows", "cols"))
    numer = jnp.sum(gradient * gradient)
    image = product(left_rows, product(gradient, right_rows.T))
    denom = lax.psum(jnp.sum(image * image), ("rows", "cols"))
    return core + numer / denom * gradient


def solution(mesh):
    return jax.shard_map(
        shards,
        mesh=mesh,
        in_specs=(P("rows", "cols"), P("rows", "cols"), P(), P("cols", "rows")),
        out_specs=P(),
        check_vma=False,
    )
```

profile of v0, /device:TPU:0, one launch (start us, length us, event | category | flops | bytes accessed | tf_op | source)
XLA Modules:
  0.0 382.8 jit_solution(6131846957028007544)
XLA Ops:
  6.5 0.0 all-gather.3.cloned.1.call-start
  6.5 0.7 all-gather.3.cloned.1.call-update
  7.3 0.0 all-gather.5.cloned.1.call-start
  7.3 0.7 all-gather.5.cloned.1.call-update
  8.0 0.0 all-reduce.2.cloned.1.call-start
  8.1 26.2 %all-gather.3.cloned.1.call-done = f32[512,1024]{1,0:T(8,128)} async-done(((f32[512,256]{1,0:T(8,128)}), f32[512,1024]{1,0:T(8,128)}) %all-gather.3.cloned.1.call-update) | async-done | bytes 2097168 | tf_op jit(solution)/shard_map/all_gather | solution.py:13
  34.2 10.2 %fusion.1 = f32[1024,512]{1,0:T(8,128)} fusion(f32[1024,1024]{1,0:T(8,128)} %param.6, f32[512,1024]{1,0:T(8,128)} %all-gather.3.cloned.1.call-done), kind=kOutput, calls=%fused_computation.6 | convolution fusion | flops 6442450944 | bytes 8388608 | tf_op jit(solution)/shard_map/dot_general | solution.py:8
  44.5 0.0 copy-start
  44.5 66.5 %all-gather.5.cloned.1.call-done = f32[1024,1024]{1,0:T(8,128)} async-done(((f32[1024,128]{1,0:T(8,128)}), f32[1024,1024]{1,0:T(8,128)}) %all-gather.5.cloned.1.call-update) | async-done | bytes 4194320 | tf_op jit(solution)/shard_map/all_gather | solution.py:12
  110.9 0.0 copy-start.3
  110.9 10.0 %fusion.2 = f32[512,1024]{0,1:T(8,128)S(1)} fusion(f32[1024,512]{1,0:T(8,128)} %fusion.1, f32[1024,1024]{1,0:T(8,128)} %all-gather.5.cloned.1.call-done), kind=kOutput, calls=%fused_computation.7 | convolution fusion | flops 6442450944 | bytes 8388608 | tf_op jit(solution)/shard_map/dot_general | solution.py:8
  120.9 0.0 copy-done
  120.9 0.0 copy-done.3
  120.9 0.0 copy-start.1
  120.9 6.9 %fusion = f32[1024,1024]{1,0:T(8,128)S(1)} fusion(f32[512,1024]{1,0:T(8,128)S(1)} %copy-done, f32[1024,512]{1,0:T(8,128)S(1)} %copy-done.3, f32[512,1024]{0,1:T(8,128)S(1)} %fusion.2), kind=kOutput, calls=%fused_computation.4 | convolution fusion | flops 6442975232 | bytes 10485760 | tf_op jit(solution)/shard_map/dot_general | solution.py:8
  127.8 0.0 copy-done.1
  127.8 14.9 %convolution_bitcast_fusion = f32[1024,1024]{0,1:T(8,128)} fusion(f32[1024,1024]{1,0:T(8,128)S(1)} %fusion, f32[1024,1024]{1,0:T(8,128)S(1)} %copy-done.1), kind=kOutput, calls=%fused_computation.2 | convolution fusion | flops 12884901888 | bytes 12582912 | tf_op jit(solution)/shard_map/dot_general | solution.py:8
  142.7 0.0 all-reduce.2.cloned.1.call-update
  142.7 140.8 %all-reduce.2.cloned.1.call-done = f32[1024,1024]{0,1:T(8,128)} async-done(((f32[1024,1024]{0,1:T(8,128)}), f32[1024,1024]{0,1:T(8,128)}) %all-reduce.2.cloned.1.call-update) | async-done | bytes 4194320 | tf_op jit(solution)/shard_map/psum | solution.py:18
  283.5 0.0 copy-start.2
  283.5 15.6 %fusion.3 = f32[1024,512]{1,0:T(8,128)S(1)} fusion(f32[1024,1024]{0,1:T(8,128)} %all-reduce.2.cloned.1.call-done, f32[512,1024]{1,0:T(8,128)S(1)} %copy-done), kind=kOutput, calls=%fused_computation.8 | convolution fusion | flops 6442450944 | bytes 8388608 | tf_op jit(solution)/shard_map/dot_general | solution.py:8
  299.2 0.0 copy-done.2
  299.2 14.3 %multiply_reduce_fusion.1 = f32[]{:T(128)} fusion(f32[1024,512]{1,0:T(8,128)S(1)} %fusion.3, f32[1024,1024]{1,0:T(8,128)S(1)} %copy-done.2), kind=kOutput, calls=%fused_computation.5 | convolution fusion | flops 6443499520 | bytes 6291460 | tf_op jit(solution)/shard_map/dot_general | solution.py:8
  313.5 5.3 %copy.5 = f32[1024,1024]{0,1:T(8,128)} copy(f32[1024,1024]{1,0:T(8,128)} %param.6) | data formatting | bytes 8388608 | tf_op args[2]
  318.9 39.5 %psum.15 = f32[]{:T(128)} all-reduce(f32[]{:T(128)} %multiply_reduce_fusion.1), channel_id=1, replica_groups=mesh['rows'=4,'cols'=8] {'rows','cols'}, use_global_device_ids=true, to_apply=%region_3.0 | all-reduce | flops 1 | bytes 8 | tf_op jit(solution)/shard_map/psum | solution.py:21
  358.3 3.9 %multiply_reduce_fusion = f32[]{:T(128)} fusion(f32[1024,1024]{0,1:T(8,128)} %all-reduce.2.cloned.1.call-done), kind=kLoop, calls=%fused_computation.1 | loop fusion | flops 2097151 | bytes 4194308 | tf_op jit(solution)/shard_map/reduce_sum | solution.py:19
  363.6 6.9 %multiply_add_fusion = f32[1024,1024]{0,1:T(8,128)} fusion(f32[1024,1024]{0,1:T(8,128)} %copy.5, f32[1024,1024]{0,1:T(8,128)} %all-reduce.2.cloned.1.call-done, f32[]{:T(128)S(6)} %div.3), kind=kLoop, calls=%fused_computation | loop fusion | flops 2097152 | bytes 12582916 | tf_op jit(solution)/shard_map/add | solution.py:22
  370.4 5.3 %copy.6 = f32[1024,1024]{1,0:T(8,128)} copy(f32[1024,1024]{0,1:T(8,128)} %multiply_add_fusion) | data formatting | bytes 8388608 | tf_op jit(solution)/shard_map/add | solution.py:22
Async XLA Ops:
  6.5 27.7 %all-gather.3.cloned.1.call-start = ((), (), s32[]{:S(2)}) async-start(), calls=%async_computation | async-start | bytes 2621440 | tf_op jit(solution)/shard_map/all_gather | solution.py:13
  7.3 103.7 %all-gather.5.cloned.1.call-start = ((), (), s32[]{:S(2)}) async-start(), calls=%async_computation.1 | async-start | bytes 4718592 | tf_op jit(solution)/shard_map/all_gather | solution.py:12
  8.0 275.5 %all-reduce.2.cloned.1.call-start = ((), (), s32[]{:S(2)}) async-start(), calls=%async_computation.2 | async-start | bytes 8388608 | tf_op jit(solution)/shard_map/psum | solution.py:18
  44.5 76.4 %copy-start = (f32[512,1024]{1,0:T(8,128)S(1)}, f32[512,1024]{1,0:T(8,128)}, u32[]{:S(2)}) copy-start(f32[512,1024]{1,0:T(8,128)} %all-gather.3.cloned.1.call-done) | copy-start | bytes 6291460
  110.9 10.0 %copy-start.3 = (f32[1024,512]{1,0:T(8,128)S(1)}, f32[1024,512]{1,0:T(8,128)}, u32[]{:S(2)}) copy-start(f32[1024,512]{1,0:T(8,128)} %param.4) | copy-start | bytes 6291460
  120.9 6.9 %copy-start.1 = (f32[1024,1024]{1,0:T(8,128)S(1)}, f32[1024,1024]{1,0:T(8,128)}, u32[]{:S(2)}) copy-start(f32[1024,1024]{1,0:T(8,128)} %all-gather.5.cloned.1.call-done) | copy-start | bytes 12582916
  283.5 15.6 %copy-start.2 = (f32[1024,1024]{1,0:T(8,128)S(1)}, f32[1024,1024]{1,0:T(8,128)}, u32[]{:S(2)}) copy-start(f32[1024,1024]{1,0:T(8,128)} %all-gather.5.cloned.1.call-done) | copy-start | bytes 12582916
Sparse Core Ops, SparseCore 0:
  8.9 25.2 all-gather.2
  36.2 74.6 all-gather.4
  142.9 140.6 all-reduce.1
where the time goes:
time: 389 us; the launch traced here: 383 us
  waiting for transfers between devices  235 us (60%)
  matrix products  72 us (19%)
  blocking collectives  39.5 us (10%)
  between operations  15 us (4%)
  other arithmetic  10.8 us (3%)
  local copies, waits for them, and re-layouts  10.7 us (3%)
    psum x1, waiting for transfers between devices, shards(): gradient = lax.psum(local_term, ('rows', 'cols'))  141 us
    dot_general x6, matrix products, product(): jnp.dot(left, right, precision=lax.Precision.HIGHEST, preferred_element_t...  72 us
    all_gather x1, waiting for transfers between devices, shards(): left_rows = lax.all_gather(left_factor, 'cols', axis=1, tiled=True)  66.5 us
    psum x1, blocking collectives, shards(): denom = lax.psum(jnp.sum(image * image), ('rows', 'cols'))  39.5 us
    all_gather x1, waiting for transfers between devices, shards(): right_rows = lax.all_gather(right_factor, 'rows', axis=1, tiled=True)  26.2 us
  transfers between devices with their start and end apart: 3, of which 3 were waited for; matrix products, arithmetic and copies ran while one was open for 3% of the time, Pallas kernels for 0%

commit v1 on v0

--- a/solution.py
+++ b/solution.py
@@ -15,7 +15,7 @@
     residual = pair_integrals - product(left_rows, mixed)
     along = product(residual, right_rows)
     local_term = product(left_rows.T, along)
-    gradient = lax.psum(local_term, ("rows", "cols"))
+    gradient = lax.psum(lax.psum(local_term, "cols"), "rows")
     numer = jnp.sum(gradient * gradient)
     image = product(left_rows, product(gradient, right_rows.T))
     denom = lax.psum(jnp.sum(image * image), ("rows", "cols"))

time: 389 us -> 490 us (1.26)
  waiting for transfers between devices: 235 us -> 335 us
    psum x1 -> x2, waiting for transfers between devices: 141 us -> 241 us  [shards(): gradient = lax.psum(lax.psum(local_term, 'cols'), 'rows')]
  transfers between devices with their start and end apart: 3 -> 4, of which waited for: 3 -> 4; matrix products, arithmetic and copies ran while one was open for 3% -> 2% of each run, Pallas kernels for 0% -> 0%
where the time goes in v1:
time: 490 us; the launch traced here: 484 us
  waiting for transfers between devices  335 us (68%)
  matrix products  72 us (15%)
  blocking collectives  39.6 us (8%)
  between operations  15 us (3%)
  other arithmetic  10.8 us (2%)
  local copies, waits for them, and re-layouts  10.7 us (2%)
    psum x2, waiting for transfers between devices, shards(): gradient = lax.psum(lax.psum(local_term, 'cols'), 'rows')  241 us
    dot_general x6, matrix products, product(): jnp.dot(left, right, precision=lax.Precision.HIGHEST, preferred_element_t...  72 us
    all_gather x1, waiting for transfers between devices, shards(): left_rows = lax.all_gather(left_factor, 'cols', axis=1, tiled=True)  66.5 us
    psum x1, blocking collectives, shards(): denom = lax.psum(jnp.sum(image * image), ('rows', 'cols'))  39.6 us
    all_gather x1, waiting for transfers between devices, shards(): right_rows = lax.all_gather(right_factor, 'rows', axis=1, tiled=True)  26.2 us
  transfers between devices with their start and end apart: 4, of which 4 were waited for; matrix products, arithmetic and copies ran while one was open for 2% of the time, Pallas kernels for 0%

profile of v1, /device:TPU:0, one launch (start us, length us, event | category | flops | bytes accessed | tf_op | source)
XLA Modules:
  0.0 483.5 jit_solution(4981012401085414892)
XLA Ops:
  6.5 0.0 all-gather.3.cloned.1.call-start
  6.5 0.7 all-gather.3.cloned.1.call-update
  7.3 0.0 all-gather.5.cloned.1.call-start
  7.3 0.7 all-gather.5.cloned.1.call-update
  8.0 0.0 all-reduce.3.cloned.1.call-start
  8.1 26.2 %all-gather.3.cloned.1.call-done = f32[512,1024]{1,0:T(8,128)} async-done(((f32[512,256]{1,0:T(8,128)}), f32[512,1024]{1,0:T(8,128)}) %all-gather.3.cloned.1.call-update) | async-done | bytes 2097168 | tf_op jit(solution)/shard_map/all_gather | solution.py:13
  34.2 10.2 %fusion.1 = f32[1024,512]{1,0:T(8,128)} fusion(f32[1024,1024]{1,0:T(8,128)} %param.6, f32[512,1024]{1,0:T(8,128)} %all-gather.3.cloned.1.call-done), kind=kOutput, calls=%fused_computation.6 | convolution fusion | flops 6442450944 | bytes 8388608 | tf_op jit(solution)/shard_map/dot_general | solution.py:8
  44.5 0.0 copy-start
  44.5 66.5 %all-gather.5.cloned.1.call-done = f32[1024,1024]{1,0:T(8,128)} async-done(((f32[1024,128]{1,0:T(8,128)}), f32[1024,1024]{1,0:T(8,128)}) %all-gather.5.cloned.1.call-update) | async-done | bytes 4194320 | tf_op jit(solution)/shard_map/all_gather | solution.py:12
  110.9 0.0 copy-start.3
  110.9 10.0 %fusion.2 = f32[512,1024]{0,1:T(8,128)S(1)} fusion(f32[1024,512]{1,0:T(8,128)} %fusion.1, f32[1024,1024]{1,0:T(8,128)} %all-gather.5.cloned.1.call-done), kind=kOutput, calls=%fused_computation.7 | convolution fusion | flops 6442450944 | bytes 8388608 | tf_op jit(solution)/shard_map/dot_general | solution.py:8
  120.9 0.0 copy-done
  120.9 0.0 copy-done.3
  120.9 0.0 copy-start.1
  120.9 6.9 %fusion = f32[1024,1024]{1,0:T(8,128)S(1)} fusion(f32[512,1024]{1,0:T(8,128)S(1)} %copy-done, f32[1024,512]{1,0:T(8,128)S(1)} %copy-done.3, f32[512,1024]{0,1:T(8,128)S(1)} %fusion.2), kind=kOutput, calls=%fused_computation.4 | convolution fusion | flops 6442975232 | bytes 10485760 | tf_op jit(solution)/shard_map/dot_general | solution.py:8
  127.8 0.0 copy-done.1
  127.8 14.9 %convolution_bitcast_fusion = f32[1024,1024]{0,1:T(8,128)} fusion(f32[1024,1024]{1,0:T(8,128)S(1)} %fusion, f32[1024,1024]{1,0:T(8,128)S(1)} %copy-done.1), kind=kOutput, calls=%fused_computation.2 | convolution fusion | flops 12884901888 | bytes 12582912 | tf_op jit(solution)/shard_map/dot_general | solution.py:8
  142.7 0.0 all-reduce.3.cloned.1.call-update
  142.7 0.0 all-reduce.5.cloned.1.call-start
  142.8 154.6 %all-reduce.3.cloned.1.call-done = f32[1024,1024]{0,1:T(8,128)} async-done(((f32[1024,1024]{0,1:T(8,128)}), f32[1024,1024]{0,1:T(8,128)}) %all-reduce.3.cloned.1.call-update) | async-done | bytes 4194320 | tf_op jit(solution)/shard_map/psum | solution.py:18
  297.4 0.0 all-reduce.5.cloned.1.call-update
  297.5 86.7 %all-reduce.5.cloned.1.call-done = f32[1024,1024]{0,1:T(8,128)} async-done(((f32[1024,1024]{0,1:T(8,128)}), f32[1024,1024]{0,1:T(8,128)}) %all-reduce.5.cloned.1.call-update) | async-done | bytes 4194320 | tf_op jit(solution)/shard_map/psum | solution.py:18
  384.2 0.0 copy-start.2
  384.2 15.6 %fusion.3 = f32[1024,512]{1,0:T(8,128)S(1)} fusion(f32[1024,1024]{0,1:T(8,128)} %all-reduce.5.cloned.1.call-done, f32[512,1024]{1,0:T(8,128)S(1)} %copy-done), kind=kOutput, calls=%fused_computation.8 | convolution fusion | flops 6442450944 | bytes 8388608 | tf_op jit(solution)/shard_map/dot_general | solution.py:8
  399.8 0.0 copy-done.2
  399.8 14.3 %multiply_reduce_fusion.1 = f32[]{:T(128)} fusion(f32[1024,512]{1,0:T(8,128)S(1)} %fusion.3, f32[1024,1024]{1,0:T(8,128)S(1)} %copy-done.2), kind=kOutput, calls=%fused_computation.5 | convolution fusion | flops 6443499520 | bytes 6291460 | tf_op jit(solution)/shard_map/dot_general | solution.py:8
  414.1 5.3 %copy.5 = f32[1024,1024]{0,1:T(8,128)} copy(f32[1024,1024]{1,0:T(8,128)} %param.6) | data formatting | bytes 8388608 | tf_op args[2]
  419.5 39.6 %psum.23 = f32[]{:T(128)} all-reduce(f32[]{:T(128)} %multiply_reduce_fusion.1), channel_id=1, replica_groups=mesh['rows'=4,'cols'=8] {'rows','cols'}, use_global_device_ids=true, to_apply=%region_4.0 | all-reduce | flops 1 | bytes 8 | tf_op jit(solution)/shard_map/psum | solution.py:21
  459.0 3.9 multiply_reduce_fusion
  464.3 6.9 %multiply_add_fusion = f32[1024,1024]{0,1:T(8,128)} fusion(f32[1024,1024]{0,1:T(8,128)} %copy.5, f32[1024,1024]{0,1:T(8,128)} %all-reduce.5.cloned.1.call-done, f32[]{:T(128)S(6)} %div.3), kind=kLoop, calls=%fused_computation | loop fusion | flops 2097152 | bytes 12582916 | tf_op jit(solution)/shard_map/add | solution.py:22
  471.2 5.3 %copy.6 = f32[1024,1024]{1,0:T(8,128)} copy(f32[1024,1024]{0,1:T(8,128)} %multiply_add_fusion) | data formatting | bytes 8388608 | tf_op jit(solution)/shard_map/add | solution.py:22
Async XLA Ops:
  6.5 27.7 %all-gather.3.cloned.1.call-start = ((), (), s32[]{:S(2)}) async-start(), calls=%async_computation | async-start | bytes 2621440 | tf_op jit(solution)/shard_map/all_gather | solution.py:13
  7.3 103.7 %all-gather.5.cloned.1.call-start = ((), (), s32[]{:S(2)}) async-start(), calls=%async_computation.1 | async-start | bytes 4718592 | tf_op jit(solution)/shard_map/all_gather | solution.py:12
  8.0 289.4 %all-reduce.3.cloned.1.call-start = ((), (), s32[]{:S(2)}) async-start(), calls=%async_computation.2 | async-start | bytes 8388608 | tf_op jit(solution)/shard_map/psum | solution.py:18
  44.5 76.4 %copy-start = (f32[512,1024]{1,0:T(8,128)S(1)}, f32[512,1024]{1,0:T(8,128)}, u32[]{:S(2)}) copy-start(f32[512,1024]{1,0:T(8,128)} %all-gather.3.cloned.1.call-done) | copy-start | bytes 6291460
  110.9 10.0 %copy-start.3 = (f32[1024,512]{1,0:T(8,128)S(1)}, f32[1024,512]{1,0:T(8,128)}, u32[]{:S(2)}) copy-start(f32[1024,512]{1,0:T(8,128)} %param.4) | copy-start | bytes 6291460
  120.9 6.9 %copy-start.1 = (f32[1024,1024]{1,0:T(8,128)S(1)}, f32[1024,1024]{1,0:T(8,128)}, u32[]{:S(2)}) copy-start(f32[1024,1024]{1,0:T(8,128)} %all-gather.5.cloned.1.call-done) | copy-start | bytes 12582916
  142.7 241.4 %all-reduce.5.cloned.1.call-start = ((), (), s32[]{:S(2)}) async-start(), calls=%async_computation.3 | async-start | bytes 8388608 | tf_op jit(solution)/shard_map/psum | solution.py:18
  384.2 15.6 %copy-start.2 = (f32[1024,1024]{1,0:T(8,128)S(1)}, f32[1024,1024]{1,0:T(8,128)}, u32[]{:S(2)}) copy-start(f32[1024,1024]{1,0:T(8,128)} %all-gather.5.cloned.1.call-done) | copy-start | bytes 12582916
Sparse Core Ops, SparseCore 0:
  8.9 25.2 all-gather.2
  36.2 74.6 all-gather.4
  142.9 154.5 all-reduce.2
  299.7 84.4 all-reduce.4
